TPU v7x, 32 devices: a whole 2x2x4 slice. The times are simulated.
32 devices in a mesh: dp: 4 (over z), tensor: 8 (over y, x, core).
Axes of the slice: x: 2, y: 2, z: 4, core: 2. Of those that a mesh axis runs over, the one named last changes fastest.
Arguments:
- activations: bfloat16 [3072, 4096], P('dp', 'tensor'), may hold values from -6 to 6
- out_grads_t: bfloat16 [5504, 3072], P('tensor', 'dp'), may hold values from -6 to 6
- in_basis: bfloat16 [4096, 4096], P(None, 'tensor'), may hold values from -0.09375 to 0.09375
- out_basis_t: bfloat16 [5504, 5504], P('tensor'), may hold values from -0.078125 to 0.078125
- query_proj: bfloat16 [4, 5504, 4096], P(None, 'tensor', 'dp'), may hold values from -6 to 6
- eigvals: float32 [5504, 4096], P('tensor', 'dp'), may hold values from 0.05 to 5
- damping: float32 [1], replicated, may hold values from 0.05 to 0.2
- lengths: int32 [24], P('dp'), may hold values from 1 to 128, 1920 in all
Outputs:
- scores: float32 [24, 4], P('dp')
Inputs may be any that keep to these rules, and one draw needn't show every extreme that they name: `lengths`: the largest token count is exactly 128.
All inputs are finite; a program needn't handle non-finite values. No bound on the sum of `lengths` on one device may be relied on, other than what follows from the above.
Results may differ from a plain program's by a relative error of at most 0.006.
Values may be sent and summed in bfloat16 or wider, within the bound.
A program may use at most 128 MiB of HBM per device.

v0:
```python
import jax
import jax.numpy as jnp
from jax import lax
from jax.sharding import PartitionSpec as P


def local(activations, out_grads_t, in_basis, out_basis_t, query_proj, eigvals, damping, lengths):
    bf16, f32 = (jnp.bfloat16, jnp.float32)
    seq_count = lengths.shape[0]
    full_act = lax.all_gather(activations, "tensor", axis=1, tiled=True)
    token_rows = full_act.shape[0]
    seq_len = token_rows // seq_count
    act_local = jnp.dot(full_act, in_basis, preferred_element_type=f32).astype(bf16)
    act_full = lax.all_gather(act_local, "tensor", axis=1, tiled=True)
    features = act_full.shape[1]
    act_proj = lax.all_to_all(act_full, "dp", split_axis=1, concat_axis=0, tiled=True)
    grad_full = jnp.dot(
        out_basis_t,
        lax.all_gather(out_grads_t, "tensor", axis=0, tiled=True),
        preferred_element_type=f32,
    )
    position = lax.broadcasted_iota(jnp.int32, (seq_count, seq_len), 1)
    keep = (position < lengths[:, None]).astype(f32).reshape(1, token_rows)
    grad_local = (grad_full * keep).astype(bf16)
    grad_proj = lax.all_gather(grad_local, "dp", axis=1, tiled=True)
    scaled = (query_proj.astype(f32) / (eigvals + damping[0])).astype(bf16)
    mixed = jnp.einsum("td,qjd->qjt", act_proj, scaled, preferred_element_type=f32)
    weighted = mixed * grad_proj.astype(f32)[None, :, :]
    query_count, width, tokens = weighted.shape
    partial_value = jnp.sum(
        weighted.reshape(query_count, width, tokens // seq_len, seq_len), axis=(1, 3)
    ).T
    totals = lax.psum(partial_value, ("dp", "tensor"))
    mine = lax.dynamic_slice_in_dim(totals, lax.axis_index("dp") * seq_count, seq_count, 0)
    norm_factor = (features * out_basis_t.shape[1] * seq_len) ** (-0.5)
    return mine * norm_factor


def solution(mesh):
    placed = (
        P("dp", "tensor"),
        P("tensor", "dp"),
        P(None, "tensor"),
        P("tensor", None),
        P(None, "tensor", "dp"),
        P("tensor", "dp"),
        P(),
        P("dp"),
    )
    return jax.shard_map(
        local, mesh=mesh, in_specs=placed, out_specs=P("dp", None), check_vma=False
    )
```

profile of v0, /device:TPU:0, one launch (start us, length us, event | category | flops | bytes accessed | tf_op | source)
XLA Modules:
  0.0 405.4 jit_solution(16750571598699061149)
XLA Ops:
  6.5 0.0 all-gather.5.cloned.1.call-start
  6.5 0.7 all-gather.5.cloned.1.call-update
  7.3 0.0 all-gather.7.cloned.1.call-start
  7.3 51.2 %all-gather.5.cloned.1.call-done = bf16[768,4096]{1,0:T(8,128)(2,1)} async-done(((bf16[768,512]{1,0:T(8,128)(2,1)}), bf16[768,4096]{1,0:T(8,128)(2,1)}) %all-gather.5.cloned.1.call-update) | async-done | bytes 6291472 | tf_op jit(solution)/shard_map/all_gather | solution.py:10
  58.5 8.3 %convolution_convert_fusion = bf16[768,512]{1,0:T(8,128)(2,1)} fusion(bf16[768,4096]{1,0:T(8,128)(2,1)} %all-gather.5.cloned.1.call-done, bf16[4096,512]{1,0:T(8,128)(2,1)} %param.10), kind=kOutput, calls=%fused_computation.6 | convolution fusion | flops 3221618688 | bytes 11272192 | tf_op jit(solution)/shard_map/dot_general | solution.py:13
  66.8 0.0 all-gather.7.cloned.1.call-update
  66.9 0.0 all-gather.9.cloned.1.call-start
  66.9 0.7 all-gather.9.cloned.1.call-update
  67.6 46.0 %all-gather.7.cloned.1.call-done = bf16[768,4096]{1,0:T(8,128)(2,1)} async-done(((bf16[768,512]{1,0:T(8,128)(2,1)}), bf16[768,4096]{1,0:T(8,128)(2,1)}) %all-gather.7.cloned.1.call-update) | async-done | bytes 6291472 | tf_op jit(solution)/shard_map/all_gather | solution.py:14
  113.6 6.3 %copy.16 = bf16[96,4,8,1024]{3,2,0,1:T(8,128)(2,1)} copy(bf16[96,4,8,1024]{3,2,1,0:T(8,128)(2,1)} %bitcast.23) | data formatting | bytes 12582912 | tf_op jit(solution)/shard_map/all_to_all | solution.py:16
  119.9 0.0 copy-start.2
  119.9 5.6 %all-to-all-start = ((bf16[768,4,1024]{2,0,1:T(8,128)(2,1)}), bf16[768,4,1024]{2,0,1:T(8,128)(2,1)}, u32[]{:S(2)}, u32[]{:S(2)}) async-start(bf16[768,4,1024]{2,0,1:T(8,128)(2,1)} %bitcast.22), calls=%async_computation | async-start | bytes 12582912 | tf_op jit(solution)/shard_map/all_to_all | solution.py:16
  125.5 0.2 all-gather.11.cloned.1.call-start
  125.8 0.0 copy-done.2
  125.8 0.1 convert_bitcast_fusion
  125.9 0.0 copy-start
  125.9 44.2 %all-gather.9.cloned.1.call-done = bf16[5504,768]{1,0:T(8,128)(2,1)} async-done(((bf16[688,768]{1,0:T(8,128)(2,1)}), bf16[5504,768]{1,0:T(8,128)(2,1)}) %all-gather.9.cloned.1.call-update) | async-done | bytes 8454160 | tf_op jit(solution)/shard_map/all_gather | solution.py:19
  170.1 11.7 %multiply_convert_fusion = bf16[688,768]{1,0:T(8,128)(2,1)} fusion(bf16[688,5504]{1,0:T(8,128)(2,1)} %param.11, bf16[5504,768]{1,0:T(8,128)(2,1)} %all-gather.9.cloned.1.call-done, f32[768]{0:T(1024)S(1)} %convert_bitcast_fusion), kind=kOutput, calls=%fused_computation.4 | convolution fusion | flops 5817507840 | bytes 17087488 | tf_op jit(solution)/shard_map/dot_general | solution.py:17
  181.8 0.0 all-gather.11.cloned.1.call-update
  182.4 0.0 copy-done
  182.4 1.9 broadcast_add_fusion
  184.3 0.0 copy-start.1
  184.3 146.2 %all-gather.11.cloned.1.call-done = bf16[688,3072]{1,0:T(8,128)(2,1)} async-done(((bf16[688,768]{1,0:T(8,128)(2,1)}), bf16[688,3072]{1,0:T(8,128)(2,1)}) %all-gather.11.cloned.1.call-update) | async-done | bytes 4227088 | tf_op jit(solution)/shard_map/all_gather | solution.py:25
  330.6 6.6 %convert_element_type.31 = f32[688,3072]{1,0:T(8,128)} convert(bf16[688,3072]{1,0:T(8,128)(2,1)} %all-gather.11.cloned.1.call-done) | non-fusion elementwise | flops 2113536 | bytes 12681216 | tf_op jit(solution)/shard_map/convert_element_type | solution.py:28
  337.1 0.0 all-to-all-done
  337.1 0.0 copy-done.1
  337.1 22.6 %multiply_reduce_fusion = f32[4,3072]{1,0:T(4,128)S(1)} fusion(f32[688,3072]{1,0:T(8,128)} %convert_element_type.31, bf16[3072,1024,1]{1,0,2:T(8,128)(2,1)} %bitcast.3, bf16[4,688,1024]{2,1,0:T(8,128)(2,1)} %param.12, f32[688,1024]{1,0:T(8,128)S(1)} %copy-done.1), kind=kOutput, calls=%fused_computation | convolution fusion | flops 17339437056 | bytes 23248896 | tf_op jit(solution)/shard_map/td,qjd->qjt/dot_general | solution.py:27
  359.8 0.1 bitcast_reduce_fusion
  359.8 38.4 %psum.7 = f32[24,4]{0,1:T(4,128)S(1)} all-reduce(f32[24,4]{0,1:T(4,128)S(1)} %bitcast.25), channel_id=1, replica_groups=mesh['dp'=4,'tensor'=8] {'dp','tensor'}, use_global_device_ids=true, to_apply=%region_2.3 | all-reduce | flops 96 | bytes 768 | tf_op jit(solution)/shard_map/psum | solution.py:33
  398.2 0.6 dynamic-slice_multiply_fusion
Async XLA Ops:
  6.5 52.0 %all-gather.5.cloned.1.call-start = ((), (), s32[]{:S(2)}) async-start(), calls=%async_computation.1 | async-start | bytes 7077888 | tf_op jit(solution)/shard_map/all_gather | solution.py:10
  7.3 106.3 %all-gather.7.cloned.1.call-start = ((), (), s32[]{:S(2)}) async-start(), calls=%async_computation.2 | async-start | bytes 7077888 | tf_op jit(solution)/shard_map/all_gather | solution.py:14
  66.9 103.2 %all-gather.9.cloned.1.call-start = ((), (), s32[]{:S(2)}) async-start(), calls=%async_computation.3 | async-start | bytes 9510912 | tf_op jit(solution)/shard_map/all_gather | solution.py:19
  119.9 5.9 %copy-start.2 = (s32[6]{0:T(128)S(1)}, s32[6]{0:T(128)}, u32[]{:S(2)}) copy-start(s32[6]{0:T(128)} %param.15) | copy-start | bytes 76
  119.9 217.2 %all-to-all-start = ((bf16[768,4,1024]{2,0,1:T(8,128)(2,1)}), bf16[768,4,1024]{2,0,1:T(8,128)(2,1)}, u32[]{:S(2)}, u32[]{:S(2)}) async-start(bf16[768,4,1024]{2,0,1:T(8,128)(2,1)} %bitcast.22), calls=%async_computation | async-start | bytes 12582912 | tf_op jit(solution)/shard_map/all_to_all | solution.py:16
  125.5 205.0 %all-gather.11.cloned.1.call-start = ((), (), s32[]{:S(2)}) async-start(), calls=%async_computation.4 | async-start | bytes 5283840 | tf_op jit(solution)/shard_map/all_gather | solution.py:25
  125.9 56.6 %copy-start = (f32[688,1024]{1,0:T(8,128)S(1)}, f32[688,1024]{1,0:T(8,128)}, u32[]{:S(2)}) copy-start(f32[688,1024]{1,0:T(8,128)} %param.13) | copy-start | bytes 8454148
  184.3 152.8 %copy-start.1 = (f32[688,1024]{1,0:T(8,128)S(1)}, f32[688,1024]{1,0:T(8,128)}, u32[]{:S(2)}) copy-start(f32[688,1024]{1,0:T(8,128)} %broadcast_add_fusion) | copy-start | bytes 8454148
Sparse Core Ops, SparseCore 0:
  9.2 49.2 all-gather.4
  67.0 46.5 all-gather.6
  115.5 54.5 all-gather.8
  181.9 148.6 all-gather.10
where the time goes:
time: 406 us; the launch traced here: 405 us
  waiting for transfers between devices  289 us (71%)
  matrix products  42.6 us (10%)
  blocking collectives  38.4 us (9%)
  between operations  13.8 us (3%)
  other arithmetic  9.29 us (2%)
  local copies, waits for them, and re-layouts  6.33 us (2%)
  starting transfers between devices  5.92 us (1%)
    all_gather x1, waiting for transfers between devices, local(): grad_proj = lax.all_gather(grad_local, 'dp', axis=1, tiled=True)  146 us
    all_gather x1, waiting for transfers between devices, local(): full_act = lax.all_gather(activations, 'tensor', axis=1, tiled=True)  51.2 us
    all_gather x1, waiting for transfers between devices, local(): act_full = lax.all_gather(act_local, 'tensor', axis=1, tiled=True)  46 us
    all_gather x1, waiting for transfers between devices, local(): lax.all_gather(out_grads_t, 'tensor', axis=0, tiled=True)  44.2 us
    psum x1, blocking collectives, local(): totals = lax.psum(partial_value, ('dp', 'tensor'))  38.4 us
    dot_general x1, matrix products, local(): jnp.einsum('td,qjd->qjt', act_proj, scaled, preferred_element_type=f32)  22.6 us
    dot_general x1, matrix products, local(): jnp.dot(out_basis_t, lax.all_gather(out_grads_t, 'tensor', axis=0, tiled=...  11.7 us
    dot_general x1, matrix products, local(): jnp.dot(full_act, in_basis, preferred_element_type=f32).astype(bf16)  8.3 us
  transfers between devices with their start and end apart: 5, of which 4 were waited for; matrix products, arithmetic and copies ran while one was open for 7% of the time, Pallas kernels for 0%

commit v1 on v0

--- a/solution.py
+++ b/solution.py
@@ -30,7 +30,9 @@
     partial_value = jnp.sum(
         weighted.reshape(query_count, width, tokens // seq_len, seq_len), axis=(1, 3)
     ).T
-    totals = lax.psum(partial_value, ("dp", "tensor"))
+    totals = partial_value
+    for axis in ("dp", "tensor"):
+        totals = lax.psum(totals, axis)
     mine = lax.dynamic_slice_in_dim(totals, lax.axis_index("dp") * seq_count, seq_count, 0)
     norm_factor = (features * out_basis_t.shape[1] * seq_len) ** (-0.5)
     return mine * norm_factor

time: 406 us -> 391 us (0.963)
  blocking collectives: 38.4 us -> 23.3 us
    psum x1 -> x2, blocking collectives: 38.4 us -> 23.3 us  [local(): totals = lax.psum(totals, axis)]
where the time goes in v1:
time: 391 us; the launch traced here: 390 us
  waiting for transfers between devices  289 us (74%)
  matrix products  42.6 us (11%)
  blocking collectives  23.3 us (6%)
  between operations  13.8 us (4%)
  other arithmetic  9.28 us (2%)
  local copies, waits for them, and re-layouts  6.33 us (2%)
  starting transfers between devices  5.93 us (2%)
    all_gather x1, waiting for transfers between devices, local(): grad_proj = lax.all_gather(grad_local, 'dp', axis=1, tiled=True)  146 us
    all_gather x1, waiting for transfers between devices, local(): full_act = lax.all_gather(activations, 'tensor', axis=1, tiled=True)  51.2 us
    all_gather x1, waiting for transfers between devices, local(): act_full = lax.all_gather(act_local, 'tensor', axis=1, tiled=True)  46 us
    all_gather x1, waiting for transfers between devices, local(): lax.all_gather(out_grads_t, 'tensor', axis=0, tiled=True)  44.2 us
    psum x2, blocking collectives, local(): totals = lax.psum(totals, axis)  23.3 us
    dot_general x1, matrix products, local(): jnp.einsum('td,qjd->qjt', act_proj, scaled, preferred_element_type=f32)  22.6 us
    dot_general x1, matrix products, local(): jnp.dot(out_basis_t, lax.all_gather(out_grads_t, 'tensor', axis=0, tiled=...  11.7 us
    dot_general x1, matrix products, local(): jnp.dot(full_act, in_basis, preferred_element_type=f32).astype(bf16)  8.28 us
  transfers between devices with their start and end apart: 5, of which 4 were waited for; matrix products, arithmetic and copies ran while one was open for 7% of the time, Pallas kernels for 0%

profile of v1, /device:TPU:0, one launch (start us, length us, event | category | flops | bytes accessed | tf_op | source)
XLA Modules:
  0.0 390.3 jit_solution(1675297651348862309)
XLA Ops:
  6.5 0.0 all-gather.5.cloned.1.call-start
  6.5 0.7 all-gather.5.cloned.1.call-update
  7.3 0.0 all-gather.7.cloned.1.call-start
  7.3 51.2 %all-gather.5.cloned.1.call-done = bf16[768,4096]{1,0:T(8,128)(2,1)} async-done(((bf16[768,512]{1,0:T(8,128)(2,1)}), bf16[768,4096]{1,0:T(8,128)(2,1)}) %all-gather.5.cloned.1.call-update) | async-done | bytes 6291472 | tf_op jit(solution)/shard_map/all_gather | solution.py:10
  58.5 8.3 %convolution_convert_fusion = bf16[768,512]{1,0:T(8,128)(2,1)} fusion(bf16[768,4096]{1,0:T(8,128)(2,1)} %all-gather.5.cloned.1.call-done, bf16[4096,512]{1,0:T(8,128)(2,1)} %param.10), kind=kOutput, calls=%fused_computation.6 | convolution fusion | flops 3221618688 | bytes 11272192 | tf_op jit(solution)/shard_map/dot_general | solution.py:13
  66.8 0.0 all-gather.7.cloned.1.call-update
  66.8 0.0 all-gather.9.cloned.1.call-start
  66.9 0.7 all-gather.9.cloned.1.call-update
  67.6 46.0 %all-gather.7.cloned.1.call-done = bf16[768,4096]{1,0:T(8,128)(2,1)} async-done(((bf16[768,512]{1,0:T(8,128)(2,1)}), bf16[768,4096]{1,0:T(8,128)(2,1)}) %all-gather.7.cloned.1.call-update) | async-done | bytes 6291472 | tf_op jit(solution)/shard_map/all_gather | solution.py:14
  113.6 6.3 %copy.16 = bf16[96,4,8,1024]{3,2,0,1:T(8,128)(2,1)} copy(bf16[96,4,8,1024]{3,2,1,0:T(8,128)(2,1)} %bitcast.23) | data formatting | bytes 12582912 | tf_op jit(solution)/shard_map/all_to_all | solution.py:16
  119.9 0.0 copy-start.2
  119.9 5.6 %all-to-all-start = ((bf16[768,4,1024]{2,0,1:T(8,128)(2,1)}), bf16[768,4,1024]{2,0,1:T(8,128)(2,1)}, u32[]{:S(2)}, u32[]{:S(2)}) async-start(bf16[768,4,1024]{2,0,1:T(8,128)(2,1)} %bitcast.22), calls=%async_computation | async-start | bytes 12582912 | tf_op jit(solution)/shard_map/all_to_all | solution.py:16
  125.5 0.2 all-gather.11.cloned.1.call-start
  125.8 0.0 copy-done.2
  125.8 0.1 convert_bitcast_fusion
  125.8 0.0 copy-start
  125.8 44.2 %all-gather.9.cloned.1.call-done = bf16[5504,768]{1,0:T(8,128)(2,1)} async-done(((bf16[688,768]{1,0:T(8,128)(2,1)}), bf16[5504,768]{1,0:T(8,128)(2,1)}) %all-gather.9.cloned.1.call-update) | async-done | bytes 8454160 | tf_op jit(solution)/shard_map/all_gather | solution.py:19
  170.0 11.7 %multiply_convert_fusion = bf16[688,768]{1,0:T(8,128)(2,1)} fusion(bf16[688,5504]{1,0:T(8,128)(2,1)} %param.11, bf16[5504,768]{1,0:T(8,128)(2,1)} %all-gather.9.cloned.1.call-done, f32[768]{0:T(1024)S(1)} %convert_bitcast_fusion), kind=kOutput, calls=%fused_computation.4 | convolution fusion | flops 5817507840 | bytes 17087488 | tf_op jit(solution)/shard_map/dot_general | solution.py:17
  181.7 0.0 all-gather.11.cloned.1.call-update
  182.4 0.0 copy-done
  182.4 1.9 broadcast_add_fusion
  184.3 0.0 copy-start.1
  184.3 146.2 %all-gather.11.cloned.1.call-done = bf16[688,3072]{1,0:T(8,128)(2,1)} async-done(((bf16[688,768]{1,0:T(8,128)(2,1)}), bf16[688,3072]{1,0:T(8,128)(2,1)}) %all-gather.11.cloned.1.call-update) | async-done | bytes 4227088 | tf_op jit(solution)/shard_map/all_gather | solution.py:25
  330.5 6.6 %convert_element_type.31 = f32[688,3072]{1,0:T(8,128)} convert(bf16[688,3072]{1,0:T(8,128)(2,1)} %all-gather.11.cloned.1.call-done) | non-fusion elementwise | flops 2113536 | bytes 12681216 | tf_op jit(solution)/shard_map/convert_element_type | solution.py:28
  337.1 0.0 all-to-all-done
  337.1 0.0 copy-done.1
  337.1 22.6 %multiply_reduce_fusion = f32[4,3072]{1,0:T(4,128)S(1)} fusion(f32[688,3072]{1,0:T(8,128)} %convert_element_type.31, bf16[3072,1024,1]{1,0,2:T(8,128)(2,1)} %bitcast.3, bf16[4,688,1024]{2,1,0:T(8,128)(2,1)} %param.12, f32[688,1024]{1,0:T(8,128)S(1)} %copy-done.1), kind=kOutput, calls=%fused_computation | convolution fusion | flops 17339437056 | bytes 23248896 | tf_op jit(solution)/shard_map/td,qjd->qjt/dot_general | solution.py:27
  359.7 0.1 bitcast_reduce_fusion
  359.8 11.5 %psum.14 = f32[24,4]{0,1:T(4,128)S(1)} all-reduce(f32[24,4]{0,1:T(4,128)S(1)} %bitcast.25), channel_id=1, replica_groups=mesh['dp'=4,'tensor'=8] {'dp'}, use_global_device_ids=true, to_apply=%region_2.0 | all-reduce | flops 96 | bytes 768 | tf_op jit(solution)/shard_map/psum | solution.py:35
  371.3 11.8 %psum.15 = f32[24,4]{0,1:T(4,128)S(1)} all-reduce(f32[24,4]{0,1:T(4,128)S(1)} %psum.14), channel_id=1, replica_groups=mesh['dp'=4,'tensor'=8] {'tensor'}, use_global_device_ids=true, to_apply=%region_3.4 | all-reduce | flops 96 | bytes 768 | tf_op jit(solution)/shard_map/psum | solution.py:35
  383.1 0.7 dynamic-slice_multiply_fusion
Async XLA Ops:
  6.5 52.0 %all-gather.5.cloned.1.call-start = ((), (), s32[]{:S(2)}) async-start(), calls=%async_computation.1 | async-start | bytes 7077888 | tf_op jit(solution)/shard_map/all_gather | solution.py:10
  7.3 106.3 %all-gather.7.cloned.1.call-start = ((), (), s32[]{:S(2)}) async-start(), calls=%async_computation.2 | async-start | bytes 7077888 | tf_op jit(solution)/shard_map/all_gather | solution.py:14
  66.8 103.2 %all-gather.9.cloned.1.call-start = ((), (), s32[]{:S(2)}) async-start(), calls=%async_computation.3 | async-start | bytes 9510912 | tf_op jit(solution)/shard_map/all_gather | solution.py:19
  119.9 5.9 %copy-start.2 = (s32[6]{0:T(128)S(1)}, s32[6]{0:T(128)}, u32[]{:S(2)}) copy-start(s32[6]{0:T(128)} %param.15) | copy-start | bytes 76
  119.9 217.2 %all-to-all-start = ((bf16[768,4,1024]{2,0,1:T(8,128)(2,1)}), bf16[768,4,1024]{2,0,1:T(8,128)(2,1)}, u32[]{:S(2)}, u32[]{:S(2)}) async-start(bf16[768,4,1024]{2,0,1:T(8,128)(2,1)} %bitcast.22), calls=%async_computation | async-start | bytes 12582912 | tf_op jit(solution)/shard_map/all_to_all | solution.py:16
  125.5 205.0 %all-gather.11.cloned.1.call-start = ((), (), s32[]{:S(2)}) async-start(), calls=%async_computation.4 | async-start | bytes 5283840 | tf_op jit(solution)/shard_map/all_gather | solution.py:25
  125.8 56.6 %copy-start = (f32[688,1024]{1,0:T(8,128)S(1)}, f32[688,1024]{1,0:T(8,128)}, u32[]{:S(2)}) copy-start(f32[688,1024]{1,0:T(8,128)} %param.13) | copy-start | bytes 8454148
  184.3 152.8 %copy-start.1 = (f32[688,1024]{1,0:T(8,128)S(1)}, f32[688,1024]{1,0:T(8,128)}, u32[]{:S(2)}) copy-start(f32[688,1024]{1,0:T(8,128)} %broadcast_add_fusion) | copy-start | bytes 8454148
Sparse Core Ops, SparseCore 0:
  9.2 49.2 all-gather.4
  67.0 46.5 all-gather.6
  115.5 54.5 all-gather.8
  181.9 148.6 all-gather.10
